TPU v7x, 32 devices: a whole 2x2x4 slice. The times are simulated.
32 devices in a mesh: row: 2 (over core), col: 16 (over z, y, x).
Axes of the slice: x: 2, y: 2, z: 4, core: 2. Of those that a mesh axis runs over, the one named last changes fastest.
Arguments:
- mat_a: bfloat16 [5120, 24576], P('row', 'col'), may hold values from -6 to 6
- mat_b: bfloat16 [24576, 4096], P('row', 'col'), may hold values from -0.15625 to 0.15625
- mask_a: int32 [40, 192], P('row', 'col'), may hold values from 0 to 1, as said below
- mask_b: int32 [192, 32], P('row', 'col'), may hold values 0 or 1
Outputs:
- product: bfloat16 [5120, 4096], P('row', 'col')
Inputs may be any that keep to these rules, and one draw needn't show every extreme that they name: `mask_a`: in each tile of 20 x 12 entries, the block rows holding an occupied block come first and each holds at least one; in every draw some tile has all 20 block rows occupied.
All inputs are finite; a program needn't handle non-finite values. No bound on the sum of `mask_b` on one device may be relied on, other than what follows from the above.
Results may differ from a plain program's by a relative error of at most 0.0025.
Values may be sent and summed in bfloat16 or wider, within the bound.
A program may use at most 128 MiB of HBM per device.

v0:
```python
import functools

import jax
import jax.numpy as jnp
from jax import lax
from jax.experimental import pallas as pl
from jax.experimental.pallas import tpu as pltpu
from jax.sharding import PartitionSpec as P

BLK = 128
LEVELS = 32767.0
TINY = 1e-33
MESH = pl.DeviceIdType.MESH


def times_flag(block, flag):
    scale = jnp.full(block.shape, flag.astype(jnp.float32)).astype(block.dtype)
    return block * scale


def kernel(
    group,
    a_hbm, b_hbm, flags_a, flags_b, out_ref,
    a_tile, b_own, b_raw, b_send, b_recv, own_sum, code_send, code_recv, step_send, step_recv,
    a_sem, b_sem, bs_sem, br_sem, cs_sem, cr_sem, ss_sem, sr_sem,
):
    n_row, n_col = lax.axis_size("row"), lax.axis_size("col")
    row, col = lax.axis_index("row"), lax.axis_index("col")
    up, down = lax.rem(row + n_row - 1, n_row), lax.rem(row + 1, n_row)
    left, right = lax.rem(col + n_col - 1, n_col), lax.rem(col + 1, n_col)
    rows, inner = a_tile.shape
    width = b_own.shape[1]
    deep, halves = inner // BLK, width // BLK
    span = group * BLK
    chunks = rows // span

    def piece(c):
        return pl.ds(pl.multiple_of(c * span, span), span)

    def load_a(c):
        return pltpu.make_async_copy(a_hbm.at[piece(c), :], a_tile.at[piece(c), :], a_sem.at[c])

    slot = jnp.where(row == 0, 1, 0)
    get_send = pltpu.make_async_copy(
        b_hbm.at[pl.ds(pl.multiple_of(slot * inner, inner), inner), :], b_raw, b_sem.at[0]
    )
    get_own = pltpu.make_async_copy(b_hbm.at[pl.ds(0, inner), :], b_own, b_sem.at[1])

    barrier = pltpu.get_barrier_semaphore()
    pl.semaphore_signal(barrier, inc=1, device_id={"row": down, "col": left}, device_id_type=MESH)
    pl.semaphore_signal(barrier, inc=1, device_id={"row": row, "col": right}, device_id_type=MESH)
    get_send.start()
    get_own.start()
    for c in range(chunks):
        load_a(c).start()

    get_send.wait()
    for h in range(halves):
        for k in range(deep):
            block = b_raw[k * BLK:(k + 1) * BLK, h * BLK:(h + 1) * BLK]
            b_send[h, k * BLK:(k + 1) * BLK, :] = times_flag(block, flags_b[h, slot * deep + k])

    def move_b(h):
        return pltpu.make_async_remote_copy(
            src_ref=b_send.at[h], dst_ref=b_recv.at[h], send_sem=bs_sem.at[h], recv_sem=br_sem.at[h],
            device_id={"row": up, "col": right}, device_id_type=MESH,
        )

    pl.semaphore_wait(barrier, 2)
    for h in range(halves):
        move_b(h).start()

    get_own.wait()
    for h in range(halves):
        for k in range(deep):
            spot = (slice(k * BLK, (k + 1) * BLK), slice(h * BLK, (h + 1) * BLK))
            b_own[spot] = times_flag(b_own[spot], flags_b[h, k])

    def own_part(c, carry):
        load_a(c).wait()
        for g in range(group):
            lines = pl.ds(pl.multiple_of(c * span + g * BLK, BLK), BLK)
            for k in range(deep):
                block = a_tile[lines, k * BLK:(k + 1) * BLK]
                a_tile[lines, k * BLK:(k + 1) * BLK] = times_flag(block, flags_a[k, c * group + g])
        own_sum[piece(c), :] = jnp.dot(a_tile[piece(c), :], b_own[...], preferred_element_type=jnp.float32)
        return carry

    lax.fori_loop(0, chunks, own_part, 0)

    def move_code(i):
        return pltpu.make_async_remote_copy(
            src_ref=code_send.at[i], dst_ref=code_recv.at[i], send_sem=cs_sem.at[i], recv_sem=cr_sem.at[i],
            device_id={"row": row, "col": left}, device_id_type=MESH,
        )

    def move_step(i):
        return pltpu.make_async_remote_copy(
            src_ref=step_send.at[i], dst_ref=step_recv.at[i], send_sem=ss_sem.at[i], recv_sem=sr_sem.at[i],
            device_id={"row": row, "col": left}, device_id_type=MESH,
        )

    def send_out(i, carry):
        move_step(i).start()
        move_code(i).start()
        return carry

    def next_part(h, early, c, carry):
        i = h * chunks + c
        value = jnp.dot(a_tile[piece(c), :], b_recv[h], preferred_element_type=jnp.float32)
        most = jnp.maximum(jnp.max(jnp.abs(value), axis=0, keepdims=True), TINY)
        step_send[i] = jnp.broadcast_to(most * (1.0 / LEVELS), step_send.shape[1:])
        code_send[i] = jnp.round(value * (LEVELS / most)).astype(jnp.int32).astype(jnp.int16)
        return carry if early else send_out(i, carry)

    for h in range(halves):
        move_b(h).wait_recv()
        if h == halves - 1:
            lax.fori_loop(0, h * chunks, send_out, 0)
        lax.fori_loop(0, chunks, functools.partial(next_part, h, h < halves - 1), 0)

    for h in range(halves):

        def finish(c, carry, h=h):
            i = h * chunks + c
            move_step(i).wait_recv()
            move_code(i).wait_recv()
            code = code_recv[i].astype(jnp.int32).astype(jnp.float32)
            total = own_sum[piece(c), h * BLK:(h + 1) * BLK] + code * step_recv[i, 0:1, :]
            out_ref[piece(c), h * BLK:(h + 1) * BLK] = total.astype(out_ref.dtype)
            return carry

        lax.fori_loop(0, chunks, finish, 0)

    for h in range(halves):
        move_b(h).wait_send()

    def sent(i, carry):
        move_step(i).wait_send()
        move_code(i).wait_send()
        return carry

    lax.fori_loop(0, halves * chunks, sent, 0)


def hand_on(pieces, source, target, held, in_sem, out_sem):
    span = source.shape[0] // pieces

    def fetch(n):
        return pltpu.make_async_copy(source.at[n * span:(n + 1) * span, :], held.at[n], in_sem.at[n])

    def put(n):
        return pltpu.make_async_copy(held.at[n], target.at[n * span:(n + 1) * span, :], out_sem.at[n])

    for n in range(pieces):
        fetch(n).start()
    for n in range(pieces):
        fetch(n).wait()
        put(n).start()
    for n in range(pieces):
        put(n).wait()


def body(mat_a, mat_b, mask_a, mask_b):
    rows, inner = mat_a.shape
    width = mat_b.shape[1]
    block_rows = mask_a.shape[0]
    group = next(g for g in (4, 2, 1) if block_rows % g == 0)
    span = group * BLK
    chunks = rows // span
    halves = width // BLK
    sends = halves * chunks
    dma = pltpu.SemaphoreType.DMA
    product = pl.pallas_call(
        functools.partial(kernel, group),
        out_shape=jax.ShapeDtypeStruct((rows, width), jnp.bfloat16),
        in_specs=[
            pl.BlockSpec(memory_space=pl.ANY),
            pl.BlockSpec(memory_space=pl.ANY),
            pl.BlockSpec(memory_space=pltpu.SMEM),
            pl.BlockSpec(memory_space=pltpu.SMEM),
        ],
        out_specs=pl.BlockSpec(memory_space=pltpu.VMEM),
        scratch_shapes=[
            pltpu.VMEM((rows, inner), jnp.bfloat16),
            pltpu.VMEM((inner, width), jnp.bfloat16),
            pltpu.VMEM((inner, width), jnp.bfloat16),
            pltpu.VMEM((halves, inner, BLK), jnp.bfloat16),
            pltpu.VMEM((halves, inner, BLK), jnp.bfloat16),
            pltpu.VMEM((rows, width), jnp.float32),
            pltpu.VMEM((sends, span, BLK), jnp.int16),
            pltpu.VMEM((sends, span, BLK), jnp.int16),
            pltpu.VMEM((sends, 8, BLK), jnp.float32),
            pltpu.VMEM((sends, 8, BLK), jnp.float32),
            dma((chunks,)), dma((2,)), dma((halves,)), dma((halves,)),
            dma((sends,)), dma((sends,)), dma((sends,)), dma((sends,)),
        ],
        compiler_params=pltpu.CompilerParams(collective_id=0, has_side_effects=True),
        name="cannon",
    )(mat_a, mat_b, mask_a.T, mask_b.T)
    pieces = chunks
    return pl.pallas_call(
        functools.partial(hand_on, pieces),
        out_shape=jax.ShapeDtypeStruct(product.shape, product.dtype),
        in_specs=[pl.BlockSpec(memory_space=pl.ANY)],
        out_specs=pl.BlockSpec(memory_space=pl.ANY),
        scratch_shapes=[
            pltpu.VMEM((pieces, rows // pieces, width), product.dtype),
            dma((pieces,)), dma((pieces,)),
        ],
        name="hand_on",
    )(product)


def solution(mesh):
    return jax.shard_map(
        body,
        mesh=mesh,
        in_specs=(P("row", "col"), P("row", "col"), P("row", "col"), P("row", "col")),
        out_specs=P("row", "col"),
        check_vma=False,
    )
```

profile of v0, /device:TPU:0, one launch (start us, length us, event | category | flops | bytes accessed | tf_op | source)
XLA Modules:
  0.0 61.1 jit_solution(4332359890618979076)
XLA Ops:
  0.0 59.0 %cannon.1.source = bf16[2560,256]{1,0:T(8,128)(2,1)} custom-call(bf16[2560,1536]{1,0:T(8,128)(2,1)} %a_hbm.1, bf16[12288,256]{1,0:T(8,128)(2,1)} %b_hbm.1, s32[12,20]{1,0:T(8,128)} %bitcast.2, s32[2,96]{1,0:T(2,128)} %bitcast.3), custom_call_target="tpu_custom_call" | custom-call | tf_op jit(solution)/shard_map/cannon/pallas_call | solution.py:174
  59.1 2.1 %hand_on.1 = bf16[2560,256]{1,0:T(8,128)(2,1)} custom-call(bf16[2560,256]{1,0:T(8,128)(2,1)} %cannon.1.source), custom_call_target="tpu_custom_call" | custom-call | tf_op jit(solution)/shard_map/hand_on/pallas_call | solution.py:202
where the time goes:
time: 61.4 us; the launch traced here: 61.1 us
  Pallas kernels  61.1 us (100%)
    pallas_call x1, Pallas kernels, body(): pl.pallas_call(functools.partial(kernel, group), out_shape=jax.ShapeDtype...  59 us
    pallas_call x1, Pallas kernels, body(): pl.pallas_call(functools.partial(hand_on, pieces), out_shape=jax.ShapeDty...  2.08 us

commit v1 on v0

--- a/solution.py
+++ b/solution.py
@@ -20,9 +20,9 @@
 
 def kernel(
     group,
-    a_hbm, b_hbm, flags_a, flags_b, out_ref,
-    a_tile, b_own, b_raw, b_send, b_recv, own_sum, code_send, code_recv, step_send, step_recv,
-    a_sem, b_sem, bs_sem, br_sem, cs_sem, cr_sem, ss_sem, sr_sem,
+    a_hbm, b_hbm, flags_a, flags_b, out_hbm,
+    a_tile, b_own, b_send, b_recv, own_sum, code_send, code_recv, step_send, step_recv, out_tile,
+    a_sem, b_sem, o_sem, bs_sem, br_sem, cs_sem, cr_sem, ss_sem, sr_sem,
 ):
     n_row, n_col = lax.axis_size("row"), lax.axis_size("col")
     row, col = lax.axis_index("row"), lax.axis_index("col")
@@ -41,24 +41,22 @@
         return pltpu.make_async_copy(a_hbm.at[piece(c), :], a_tile.at[piece(c), :], a_sem.at[c])
 
     slot = jnp.where(row == 0, 1, 0)
-    get_send = pltpu.make_async_copy(
-        b_hbm.at[pl.ds(pl.multiple_of(slot * inner, inner), inner), :], b_raw, b_sem.at[0]
-    )
-    get_own = pltpu.make_async_copy(b_hbm.at[pl.ds(0, inner), :], b_own, b_sem.at[1])
+
+    def load_send(h):
+        return pltpu.make_async_copy(
+            b_hbm.at[pl.ds(pl.multiple_of(slot * inner, inner), inner), h * BLK:(h + 1) * BLK], b_send.at[h], b_sem.at[h]
+        )
+
+    get_own = pltpu.make_async_copy(b_hbm.at[pl.ds(0, inner), :], b_own, b_sem.at[halves])
 
     barrier = pltpu.get_barrier_semaphore()
     pl.semaphore_signal(barrier, inc=1, device_id={"row": down, "col": left}, device_id_type=MESH)
-    pl.semaphore_signal(barrier, inc=1, device_id={"row": row, "col": right}, device_id_type=MESH)
-    get_send.start()
+    pl.semaphore_signal(barrier, inc=1, device_id={"row": down, "col": col}, device_id_type=MESH)
+    for h in range(halves):
+        load_send(h).start()
     get_own.start()
     for c in range(chunks):
         load_a(c).start()
-
-    get_send.wait()
-    for h in range(halves):
-        for k in range(deep):
-            block = b_raw[k * BLK:(k + 1) * BLK, h * BLK:(h + 1) * BLK]
-            b_send[h, k * BLK:(k + 1) * BLK, :] = times_flag(block, flags_b[h, slot * deep + k])
 
     def move_b(h):
         return pltpu.make_async_remote_copy(
@@ -66,8 +64,13 @@
             device_id={"row": up, "col": right}, device_id_type=MESH,
         )
 
-    pl.semaphore_wait(barrier, 2)
-    for h in range(halves):
+    for h in range(halves):
+        load_send(h).wait()
+        for k in range(deep):
+            lines = slice(k * BLK, (k + 1) * BLK)
+            b_send[h, lines, :] = times_flag(b_send[h, lines, :], flags_b[h, slot * deep + k])
+        if h == 0:
+            pl.semaphore_wait(barrier, 2)
         move_b(h).start()
 
     get_own.wait()
@@ -116,8 +119,17 @@
     for h in range(halves):
         move_b(h).wait_recv()
         if h == halves - 1:
-            lax.fori_loop(0, h * chunks, send_out, 0)
+            pass
         lax.fori_loop(0, chunks, functools.partial(next_part, h, h < halves - 1), 0)
+        if h == halves - 2:
+            for b in range(halves):
+                move_b(b).wait_send()
+            lax.fori_loop(0, (halves - 1) * chunks, send_out, 0)
+
+    def put(i, h, c):
+        return pltpu.make_async_copy(
+            out_tile.at[piece(c), h * BLK:(h + 1) * BLK], out_hbm.at[piece(c), h * BLK:(h + 1) * BLK], o_sem.at[i]
+        )
 
     for h in range(halves):
 
@@ -127,13 +139,13 @@
             move_code(i).wait_recv()
             code = code_recv[i].astype(jnp.int32).astype(jnp.float32)
             total = own_sum[piece(c), h * BLK:(h + 1) * BLK] + code * step_recv[i, 0:1, :]
-            out_ref[piece(c), h * BLK:(h + 1) * BLK] = total.astype(out_ref.dtype)
+            out_tile[piece(c), h * BLK:(h + 1) * BLK] = total.astype(out_tile.dtype)
+            put(i, h, c).start()
             return carry
 
         lax.fori_loop(0, chunks, finish, 0)
 
-    for h in range(halves):
-        move_b(h).wait_send()
+    pass
 
     def sent(i, carry):
         move_step(i).wait_send()
@@ -141,6 +153,9 @@
         return carry
 
     lax.fori_loop(0, halves * chunks, sent, 0)
+    for h in range(halves):
+        for c in range(chunks):
+            put(h * chunks + c, h, c).wait()
 
 
 def hand_on(pieces, source, target, held, in_sem, out_sem):
@@ -159,6 +174,12 @@
         put(n).start()
     for n in range(pieces):
         put(n).wait()
+
+
+def pass_on(source, target, sem):
+    copy = pltpu.make_async_copy(source, target, sem)
+    copy.start()
+    copy.wait()
 
 
 def body(mat_a, mat_b, mask_a, mask_b):
@@ -180,10 +201,9 @@
             pl.BlockSpec(memory_space=pltpu.SMEM),
             pl.BlockSpec(memory_space=pltpu.SMEM),
         ],
-        out_specs=pl.BlockSpec(memory_space=pltpu.VMEM),
+        out_specs=pl.BlockSpec(memory_space=pl.ANY),
         scratch_shapes=[
             pltpu.VMEM((rows, inner), jnp.bfloat16),
-            pltpu.VMEM((inner, width), jnp.bfloat16),
             pltpu.VMEM((inner, width), jnp.bfloat16),
             pltpu.VMEM((halves, inner, BLK), jnp.bfloat16),
             pltpu.VMEM((halves, inner, BLK), jnp.bfloat16),
@@ -192,7 +212,8 @@
             pltpu.VMEM((sends, span, BLK), jnp.int16),
             pltpu.VMEM((sends, 8, BLK), jnp.float32),
             pltpu.VMEM((sends, 8, BLK), jnp.float32),
-            dma((chunks,)), dma((2,)), dma((halves,)), dma((halves,)),
+            pltpu.VMEM((rows, width), jnp.bfloat16),
+            dma((chunks,)), dma((halves + 1,)), dma((sends,)), dma((halves,)), dma((halves,)),
             dma((sends,)), dma((sends,)), dma((sends,)), dma((sends,)),
         ],
         compiler_params=pltpu.CompilerParams(collective_id=0, has_side_effects=True),

time: 61.4 us -> 57.6 us (0.938)
  the two profiles are of different devices: /device:TPU:0 before, /device:TPU:5 now
where the time goes in v1:
time: 57.6 us; the launch traced here: 57.4 us
  Pallas kernels  57.4 us (100%)
    pallas_call x1, Pallas kernels, body(): pl.pallas_call(functools.partial(kernel, group), out_shape=jax.ShapeDtype...  55.3 us
    pallas_call x1, Pallas kernels, body(): pl.pallas_call(functools.partial(hand_on, pieces), out_shape=jax.ShapeDty...  2.08 us

profile of v1, /device:TPU:5, one launch (start us, length us, event | category | flops | bytes accessed | tf_op | source)
XLA Modules:
  0.0 57.4 jit_solution(3426581700138306861)
XLA Ops:
  0.0 55.3 %cannon.1.source = bf16[2560,256]{1,0:T(8,128)(2,1)} custom-call(bf16[2560,1536]{1,0:T(8,128)(2,1)} %a_hbm.1, bf16[12288,256]{1,0:T(8,128)(2,1)} %b_hbm.1, s32[12,20]{1,0:T(8,128)} %bitcast.2, s32[2,96]{1,0:T(2,128)} %bitcast.3), custom_call_target="tpu_custom_call" | custom-call | tf_op jit(solution)/shard_map/cannon/pallas_call | solution.py:195
  55.3 2.1 %hand_on.1 = bf16[2560,256]{1,0:T(8,128)(2,1)} custom-call(bf16[2560,256]{1,0:T(8,128)(2,1)} %cannon.1.source), custom_call_target="tpu_custom_call" | custom-call | tf_op jit(solution)/shard_map/hand_on/pallas_call | solution.py:223

commit v2 on v1

--- a/solution.py
+++ b/solution.py
@@ -19,10 +19,10 @@
 
 
 def kernel(
-    group,
-    a_hbm, b_hbm, flags_a, flags_b, out_hbm,
-    a_tile, b_own, b_send, b_recv, own_sum, code_send, code_recv, step_send, step_recv, out_tile,
-    a_sem, b_sem, o_sem, bs_sem, br_sem, cs_sem, cr_sem, ss_sem, sr_sem,
+    group, parts,
+    a_hbm, b_hbm, mask_a, mask_b, out_tile,
+    flags_a, flags_b, a_tile, b_own, b_send, b_recv, own_sum, code_send, code_recv, step_send, step_recv,
+    f_sem, a_sem, b_sem, bs_sem, br_sem, cs_sem, cr_sem, ss_sem, sr_sem,
 ):
     n_row, n_col = lax.axis_size("row"), lax.axis_size("col")
     row, col = lax.axis_index("row"), lax.axis_index("col")
@@ -33,6 +33,7 @@
     deep, halves = inner // BLK, width // BLK
     span = group * BLK
     chunks = rows // span
+    cut = inner // parts
 
     def piece(c):
         return pl.ds(pl.multiple_of(c * span, span), span)
@@ -42,36 +43,46 @@
 
     slot = jnp.where(row == 0, 1, 0)
 
-    def load_send(h):
+    def load_send(n):
+        h, p = divmod(n, parts)
         return pltpu.make_async_copy(
-            b_hbm.at[pl.ds(pl.multiple_of(slot * inner, inner), inner), h * BLK:(h + 1) * BLK], b_send.at[h], b_sem.at[h]
-        )
-
-    get_own = pltpu.make_async_copy(b_hbm.at[pl.ds(0, inner), :], b_own, b_sem.at[halves])
+            b_hbm.at[pl.ds(pl.multiple_of(slot * inner + p * cut, cut), cut), h * BLK:(h + 1) * BLK],
+            b_send.at[h, p * cut:(p + 1) * cut, :], b_sem.at[n],
+        )
+
+    get_own = pltpu.make_async_copy(b_hbm.at[pl.ds(0, inner), :], b_own, b_sem.at[halves * parts])
 
     barrier = pltpu.get_barrier_semaphore()
     pl.semaphore_signal(barrier, inc=1, device_id={"row": down, "col": left}, device_id_type=MESH)
     pl.semaphore_signal(barrier, inc=1, device_id={"row": down, "col": col}, device_id_type=MESH)
-    for h in range(halves):
-        load_send(h).start()
+    get_flags_b = pltpu.make_async_copy(mask_b, flags_b, f_sem.at[0])
+    get_flags_a = pltpu.make_async_copy(mask_a, flags_a, f_sem.at[1])
+    get_flags_b.start()
+    for n in range(halves * parts):
+        load_send(n).start()
+    get_flags_a.start()
     get_own.start()
     for c in range(chunks):
         load_a(c).start()
 
-    def move_b(h):
+    def move_b(n):
+        h, p = divmod(n, parts)
+        spot = (h, slice(p * cut, (p + 1) * cut))
         return pltpu.make_async_remote_copy(
-            src_ref=b_send.at[h], dst_ref=b_recv.at[h], send_sem=bs_sem.at[h], recv_sem=br_sem.at[h],
+            src_ref=b_send.at[spot], dst_ref=b_recv.at[spot], send_sem=bs_sem.at[n], recv_sem=br_sem.at[n],
             device_id={"row": up, "col": right}, device_id_type=MESH,
         )
 
-    for h in range(halves):
-        load_send(h).wait()
-        for k in range(deep):
+    get_flags_b.wait()
+    for n in range(halves * parts):
+        load_send(n).wait()
+        h, p = divmod(n, parts)
+        for k in range(p * deep // parts, (p + 1) * deep // parts):
             lines = slice(k * BLK, (k + 1) * BLK)
             b_send[h, lines, :] = times_flag(b_send[h, lines, :], flags_b[h, slot * deep + k])
-        if h == 0:
+        if n == 0:
             pl.semaphore_wait(barrier, 2)
-        move_b(h).start()
+        move_b(n).start()
 
     get_own.wait()
     for h in range(halves):
@@ -89,6 +100,7 @@
         own_sum[piece(c), :] = jnp.dot(a_tile[piece(c), :], b_own[...], preferred_element_type=jnp.float32)
         return carry
 
+    get_flags_a.wait()
     lax.fori_loop(0, chunks, own_part, 0)
 
     def move_code(i):
@@ -117,19 +129,15 @@
         return carry if early else send_out(i, carry)
 
     for h in range(halves):
-        move_b(h).wait_recv()
+        for n in range(h * parts, (h + 1) * parts):
+            move_b(n).wait_recv()
         if h == halves - 1:
             pass
         lax.fori_loop(0, chunks, functools.partial(next_part, h, h < halves - 1), 0)
         if h == halves - 2:
-            for b in range(halves):
-                move_b(b).wait_send()
+            for n in range(halves * parts):
+                move_b(n).wait_send()
             lax.fori_loop(0, (halves - 1) * chunks, send_out, 0)
-
-    def put(i, h, c):
-        return pltpu.make_async_copy(
-            out_tile.at[piece(c), h * BLK:(h + 1) * BLK], out_hbm.at[piece(c), h * BLK:(h + 1) * BLK], o_sem.at[i]
-        )
 
     for h in range(halves):
 
@@ -140,12 +148,14 @@
             code = code_recv[i].astype(jnp.int32).astype(jnp.float32)
             total = own_sum[piece(c), h * BLK:(h + 1) * BLK] + code * step_recv[i, 0:1, :]
             out_tile[piece(c), h * BLK:(h + 1) * BLK] = total.astype(out_tile.dtype)
-            put(i, h, c).start()
             return carry
 
         lax.fori_loop(0, chunks, finish, 0)
 
     pass
+
+    for n in range(halves * parts, halves * parts):
+        move_b(n).wait_send()
 
     def sent(i, carry):
         move_step(i).wait_send()
@@ -153,9 +163,6 @@
         return carry
 
     lax.fori_loop(0, halves * chunks, sent, 0)
-    for h in range(halves):
-        for c in range(chunks):
-            put(h * chunks + c, h, c).wait()
 
 
 def hand_on(pieces, source, target, held, in_sem, out_sem):
@@ -176,10 +183,16 @@
         put(n).wait()
 
 
-def pass_on(source, target, sem):
-    copy = pltpu.make_async_copy(source, target, sem)
-    copy.start()
-    copy.wait()
+def pass_on(pieces, source, target, sem):
+    span = source.shape[0] // pieces
+
+    def put(n):
+        return pltpu.make_async_copy(source.at[n * span:(n + 1) * span, :], target.at[n * span:(n + 1) * span, :], sem.at[n])
+
+    for n in range(pieces):
+        put(n).start()
+    for n in range(pieces):
+        put(n).wait()
 
 
 def body(mat_a, mat_b, mask_a, mask_b):
@@ -191,18 +204,22 @@
     chunks = rows // span
     halves = width // BLK
     sends = halves * chunks
+    deep = inner // BLK
+    parts = next(p for p in (4, 3, 2, 1) if deep % p == 0)
     dma = pltpu.SemaphoreType.DMA
     product = pl.pallas_call(
-        functools.partial(kernel, group),
-        out_shape=jax.ShapeDtypeStruct((rows, width), jnp.bfloat16),
+        functools.partial(kernel, group, parts),
+        out_shape=pltpu.VMEM((rows, width), jnp.bfloat16),
         in_specs=[
             pl.BlockSpec(memory_space=pl.ANY),
             pl.BlockSpec(memory_space=pl.ANY),
-            pl.BlockSpec(memory_space=pltpu.SMEM),
-            pl.BlockSpec(memory_space=pltpu.SMEM),
+            pl.BlockSpec(memory_space=pl.ANY),
+            pl.BlockSpec(memory_space=pl.ANY),
         ],
-        out_specs=pl.BlockSpec(memory_space=pl.ANY),
+        out_specs=pl.BlockSpec(memory_space=pltpu.VMEM),
         scratch_shapes=[
+            pltpu.SMEM(mask_a.shape[::-1], jnp.int32),
+            pltpu.SMEM(mask_b.shape[::-1], jnp.int32),
             pltpu.VMEM((rows, inner), jnp.bfloat16),
             pltpu.VMEM((inner, width), jnp.bfloat16),
             pltpu.VMEM((halves, inner, BLK), jnp.bfloat16),
@@ -212,24 +229,20 @@
             pltpu.VMEM((sends, span, BLK), jnp.int16),
             pltpu.VMEM((sends, 8, BLK), jnp.float32),
             pltpu.VMEM((sends, 8, BLK), jnp.float32),
-            pltpu.VMEM((rows, width), jnp.bfloat16),
-            dma((chunks,)), dma((halves + 1,)), dma((sends,)), dma((halves,)), dma((halves,)),
+            dma((2,)), dma((chunks,)), dma((halves * parts + 1,)), dma((halves * parts,)), dma((halves * parts,)),
             dma((sends,)), dma((sends,)), dma((sends,)), dma((sends,)),
         ],
-        compiler_params=pltpu.CompilerParams(collective_id=0, has_side_effects=True),
+        compiler_params=pltpu.CompilerParams(collective_id=0, has_side_effects=True, vmem_limit_bytes=55 * 1000 * 1000),
         name="cannon",
-    )(mat_a, mat_b, mask_a.T, mask_b.T)
-    pieces = chunks
+    )(mat_a, mat_b, pltpu.with_memory_space_constraint(mask_a.T, pltpu.MemorySpace.HBM), pltpu.with_memory_space_constraint(mask_b.T, pltpu.MemorySpace.HBM))
     return pl.pallas_call(
-        functools.partial(hand_on, pieces),
+        functools.partial(pass_on, chunks),
         out_shape=jax.ShapeDtypeStruct(product.shape, product.dtype),
         in_specs=[pl.BlockSpec(memory_space=pl.ANY)],
         out_specs=pl.BlockSpec(memory_space=pl.ANY),
-        scratch_shapes=[
-            pltpu.VMEM((pieces, rows // pieces, width), product.dtype),
-            dma((pieces,)), dma((pieces,)),
-        ],
-        name="hand_on",
+        scratch_shapes=[dma((chunks,))],
+        compiler_params=pltpu.CompilerParams(vmem_limit_bytes=1024 * 1024),
+        name="pass_on",
     )(product)
 
 

time: 57.6 us -> 54.2 us (0.941)
  Pallas kernels: 57.4 us -> 54 us
    pallas_call x2, Pallas kernels: 57.4 us -> 54 us  [the longest x1 52.9 us: body(): pl.pallas_call(functools.partial(kernel, group, parts), out_shape=pltpu.V...]
where the time goes in v2:
time: 54.2 us; the launch traced here: 54 us
  Pallas kernels  54 us (100%)
    pallas_call x1, Pallas kernels, body(): pl.pallas_call(functools.partial(kernel, group, parts), out_shape=pltpu.V...  52.9 us
    pallas_call x1, Pallas kernels, body(): pl.pallas_call(functools.partial(pass_on, chunks), out_shape=jax.ShapeDty...  1.09 us

profile of v2, /device:TPU:5, one launch (start us, length us, event | category | flops | bytes accessed | tf_op | source)
XLA Modules:
  0.0 54.0 jit_solution(3495685000771653928)
XLA Ops:
  0.0 52.9 %cannon.1.source = bf16[2560,256]{1,0:T(8,128)(2,1)S(1)} custom-call(bf16[2560,1536]{1,0:T(8,128)(2,1)} %a_hbm.1, bf16[12288,256]{1,0:T(8,128)(2,1)} %b_hbm.1, s32[12,20]{1,0:T(8,128)} %bitcast.2, s32[2,96]{1,0:T(2,128)} %bitcast.3), custom_call_target="tpu_custom_call" | custom-call | tf_op jit(solution)/shard_map/cannon/pallas_call | solution.py:210
  52.9 1.1 %pass_on.1 = bf16[2560,256]{1,0:T(8,128)(2,1)} custom-call(bf16[2560,256]{1,0:T(8,128)(2,1)S(1)} %cannon.1.source), custom_call_target="tpu_custom_call" | custom-call | tf_op jit(solution)/shard_map/pass_on/pallas_call | solution.py:238

commit v3 on v2

v3 whole, which is shorter than its diff:
```python
import functools

import jax
import jax.numpy as jnp
from jax import lax
from jax.experimental import pallas as pl
from jax.experimental.pallas import tpu as pltpu
from jax.sharding import PartitionSpec as P

BLK = 128
LEVELS = 32767.0
TINY = 1e-33
B_WINDOW = 3
R_WINDOW = 3
B_PARTS = (4, 3, 2, 1)
MESH = pl.DeviceIdType.MESH


def times_flag(block, flag):
    scale = jnp.full(block.shape, flag.astype(jnp.float32)).astype(block.dtype)
    return block * scale


def kernel(
    group, parts,
    a_hbm, b_hbm, mask_a, mask_b, out_tile,
    flags_a, flags_b, a_tile, b_own, b_send, b_recv, own_sum, code_send, code_recv, step_send, step_recv,
    f_sem, a_sem, b_sem, bs_sem, br_sem, cs_sem, cr_sem, ss_sem, sr_sem,
):
    n_row, n_col = lax.axis_size("row"), lax.axis_size("col")
    row, col = lax.axis_index("row"), lax.axis_index("col")
    up, down = lax.rem(row + n_row - 1, n_row), lax.rem(row + 1, n_row)
    left, right = lax.rem(col + n_col - 1, n_col), lax.rem(col + 1, n_col)
    rows, inner = a_tile.shape
    width = b_own.shape[1]
    deep, halves = inner // BLK, width // BLK
    span = group * BLK
    chunks = rows // span
    cut = inner // parts
    pieces, sends = halves * parts, halves * chunks
    ready = sends - chunks
    b_window, r_window = min(B_WINDOW, pieces), min(R_WINDOW, ready)

    def lines_of(c):
        return pl.ds(pl.multiple_of(c * span, span), span)

    def load_a(c):
        return pltpu.make_async_copy(a_hbm.at[lines_of(c), :], a_tile.at[lines_of(c), :], a_sem.at[c])

    slot = jnp.where(row == 0, 1, 0)

    def load_send(n):
        h, p = divmod(n, parts)
        return pltpu.make_async_copy(
            b_hbm.at[pl.ds(pl.multiple_of(slot * inner + p * cut, cut), cut), h * BLK:(h + 1) * BLK], b_send.at[n], b_sem.at[n]
        )

    get_own = pltpu.make_async_copy(b_hbm.at[pl.ds(0, inner), :], b_own, b_sem.at[pieces])
    get_flags_b = pltpu.make_async_copy(mask_b, flags_b, f_sem.at[0])
    get_flags_a = pltpu.make_async_copy(mask_a, flags_a, f_sem.at[1])

    def move_b(n):
        return pltpu.make_async_remote_copy(
            src_ref=b_send.at[n], dst_ref=b_recv.at[n], send_sem=bs_sem.at[n], recv_sem=br_sem.at[n],
            device_id={"row": up, "col": right}, device_id_type=MESH,
        )

    def move_code(i):
        return pltpu.make_async_remote_copy(
            src_ref=code_send.at[i], dst_ref=code_recv.at[i], send_sem=cs_sem.at[i], recv_sem=cr_sem.at[i],
            device_id={"row": row, "col": left}, device_id_type=MESH,
        )

    def move_step(i):
        return pltpu.make_async_remote_copy(
            src_ref=step_send.at[i], dst_ref=step_recv.at[i], send_sem=ss_sem.at[i], recv_sem=sr_sem.at[i],
            device_id={"row": row, "col": left}, device_id_type=MESH,
        )

    barrier = pltpu.get_barrier_semaphore()
    pl.semaphore_signal(barrier, inc=1, device_id={"row": down, "col": left}, device_id_type=MESH)
    pl.semaphore_signal(barrier, inc=1, device_id={"row": down, "col": col}, device_id_type=MESH)
    get_flags_b.start()
    for n in range(pieces):
        load_send(n).start()
    get_flags_b.wait()
    for n in range(pieces):
        load_send(n).wait()
        h, p = divmod(n, parts)
        for k in range(deep // parts):
            lines = slice(k * BLK, (k + 1) * BLK)
            b_send[n, lines, :] = times_flag(b_send[n, lines, :], flags_b[h, slot * deep + p * (deep // parts) + k])
        if n == 0:
            pl.semaphore_wait(barrier, 2)
        if n < b_window:
            move_b(n).start()
        if n == 0:
            get_flags_a.start()
            get_own.start()
            for c in range(chunks):
                load_a(c).start()

    get_own.wait()
    for h in range(halves):
        for k in range(deep):
            spot = (slice(k * BLK, (k + 1) * BLK), slice(h * BLK, (h + 1) * BLK))
            b_own[spot] = times_flag(b_own[spot], flags_b[h, k])
    get_flags_a.wait()

    def next_b(n, carry):
        move_b(n - b_window).wait_send()
        move_b(n).start()
        return carry

    def own_part(c, carry):
        load_a(c).wait()
        for g in range(group):
            lines = pl.ds(pl.multiple_of(c * span + g * BLK, BLK), BLK)
            for k in range(deep):
                block = a_tile[lines, k * BLK:(k + 1) * BLK]
                a_tile[lines, k * BLK:(k + 1) * BLK] = times_flag(block, flags_a[k, c * group + g])
        own_sum[lines_of(c), :] = jnp.dot(a_tile[lines_of(c), :], b_own[...], preferred_element_type=jnp.float32)

        @pl.when(b_window + c < pieces)
        def _():
            next_b(b_window + c, 0)

        return carry

    lax.fori_loop(0, chunks, own_part, 0)
    lax.fori_loop(min(b_window + chunks, pieces), pieces, next_b, 0)

    def send_out(i, carry):
        move_step(i).start()
        move_code(i).start()
        return carry

    def sent(i, carry):
        move_step(i).wait_send()
        move_code(i).wait_send()
        return carry

    def next_out(i, carry):
        sent(i - r_window, carry)
        return send_out(i, carry)

    def next_part(h, c, carry):
        i = h * chunks + c
        tile = b_recv[h * parts:(h + 1) * parts].reshape(inner, BLK)
        value = jnp.dot(a_tile[lines_of(c), :], tile, preferred_element_type=jnp.float32)
        most = jnp.maximum(jnp.max(jnp.abs(value), axis=0, keepdims=True), TINY)
        step_send[i] = most * (1.0 / LEVELS)
        code_send[i] = jnp.round(value * (LEVELS / most)).astype(jnp.int32).astype(jnp.int16)
        if h < halves - 1:
            return carry
        return next_out(r_window + c, carry) if r_window else send_out(c, carry)

    for h in range(halves):
        if h == halves - 1:
            for n in range(pieces - b_window, pieces):
                move_b(n).wait_send()
            lax.fori_loop(0, r_window, send_out, 0)
        for n in range(h * parts, (h + 1) * parts):
            move_b(n).wait_recv()
        lax.fori_loop(0, chunks, functools.partial(next_part, h), 0)
    if r_window:
        lax.fori_loop(r_window + chunks, sends, next_out, 0)

    for h in range(halves):

        def finish(c, carry, h=h):
            i = h * chunks + c
            move_step(i).wait_recv()
            move_code(i).wait_recv()
            code = code_recv[i].astype(jnp.int32).astype(jnp.float32)
            total = own_sum[lines_of(c), h * BLK:(h + 1) * BLK] + code * step_recv[i]
            out_tile[lines_of(c), h * BLK:(h + 1) * BLK] = total.astype(out_tile.dtype)
            return carry

        lax.fori_loop(0, chunks, finish, 0)
    lax.fori_loop(sends - r_window if r_window else 0, sends, sent, 0)


def pass_on(pieces, source, target, sem):
    span = source.shape[0] // pieces

    def put(n):
        return pltpu.make_async_copy(source.at[n * span:(n + 1) * span, :], target.at[n * span:(n + 1) * span, :], sem.at[n])

    for n in range(pieces):
        put(n).start()
    for n in range(pieces):
        put(n).wait()


def in_hbm(array):
    return pltpu.with_memory_space_constraint(array, pltpu.MemorySpace.HBM)


def body(mat_a, mat_b, mask_a, mask_b):
    rows, inner = mat_a.shape
    width = mat_b.shape[1]
    block_rows = mask_a.shape[0]
    group = next(g for g in (4, 2, 1) if block_rows % g == 0)
    parts = next(p for p in B_PARTS if inner // BLK % p == 0)
    span = group * BLK
    chunks = rows // span
    halves = width // BLK
    pieces, sends = halves * parts, halves * chunks
    dma = pltpu.SemaphoreType.DMA
    product = pl.pallas_call(
        functools.partial(kernel, group, parts),
        out_shape=pltpu.VMEM((rows, width), jnp.bfloat16),
        in_specs=[pl.BlockSpec(memory_space=pl.ANY)] * 4,
        out_specs=pl.BlockSpec(memory_space=pltpu.VMEM),
        scratch_shapes=[
            pltpu.SMEM(mask_a.shape[::-1], jnp.int32),
            pltpu.SMEM(mask_b.shape[::-1], jnp.int32),
            pltpu.VMEM((rows, inner), jnp.bfloat16),
            pltpu.VMEM((inner, width), jnp.bfloat16),
            pltpu.VMEM((pieces, inner // parts, BLK), jnp.bfloat16),
            pltpu.VMEM((pieces, inner // parts, BLK), jnp.bfloat16),
            pltpu.VMEM((rows, width), jnp.float32),
            pltpu.VMEM((sends, span, BLK), jnp.int16),
            pltpu.VMEM((sends, span, BLK), jnp.int16),
            pltpu.VMEM((sends, 1, BLK), jnp.float32),
            pltpu.VMEM((sends, 1, BLK), jnp.float32),
            dma((2,)), dma((chunks,)), dma((pieces + 1,)), dma((pieces,)), dma((pieces,)),
            dma((sends,)), dma((sends,)), dma((sends,)), dma((sends,)),
        ],
        compiler_params=pltpu.CompilerParams(collective_id=0, has_side_effects=True, vmem_limit_bytes=52 * 1024 * 1024),
        name="cannon",
    )(mat_a, mat_b, in_hbm(mask_a.T), in_hbm(mask_b.T))
    return pl.pallas_call(
        functools.partial(pass_on, chunks),
        out_shape=jax.ShapeDtypeStruct(product.shape, product.dtype),
        in_specs=[pl.BlockSpec(memory_space=pl.ANY)],
        out_specs=pl.BlockSpec(memory_space=pl.ANY),
        scratch_shapes=[dma((chunks,))],
        compiler_params=pltpu.CompilerParams(vmem_limit_bytes=1024 * 1024),
        name="pass_on",
    )(product)


def solution(mesh):
    return jax.shard_map(
        body,
        mesh=mesh,
        in_specs=(P("row", "col"), P("row", "col"), P("row", "col"), P("row", "col")),
        out_specs=P("row", "col"),
        check_vma=False,
    )
```

time: 54.2 us -> 53.4 us (0.985)
  Pallas kernels: 54 us -> 53.2 us
    pallas_call x1, Pallas kernels: 52.9 us -> 52.1 us  [body(): pl.pallas_call(functools.partial(kernel, group, parts), out_shape=pltpu.V...]
where the time goes in v3:
time: 53.4 us; the launch traced here: 53.2 us
  Pallas kernels  53.2 us (100%)
    pallas_call x1, Pallas kernels, body(): pl.pallas_call(functools.partial(kernel, group, parts), out_shape=pltpu.V...  52.1 us
    pallas_call x1, Pallas kernels, body(): pl.pallas_call(functools.partial(pass_on, chunks), out_shape=jax.ShapeDty...  1.09 us

profile of v3, /device:TPU:5, one launch (start us, length us, event | category | flops | bytes accessed | tf_op | source)
XLA Modules:
  0.0 53.2 jit_solution(3800386957012771578)
XLA Ops:
  0.0 52.1 %cannon.1.source = bf16[2560,256]{1,0:T(8,128)(2,1)S(1)} custom-call(bf16[2560,1536]{1,0:T(8,128)(2,1)} %a_hbm.1, bf16[12288,256]{1,0:T(8,128)(2,1)} %b_hbm.1, s32[12,20]{1,0:T(8,128)} %bitcast.2, s32[2,96]{1,0:T(2,128)} %bitcast.3), custom_call_target="tpu_custom_call" | custom-call | tf_op jit(solution)/shard_map/cannon/pallas_call | solution.py:211
  52.1 1.1 %pass_on.1 = bf16[2560,256]{1,0:T(8,128)(2,1)} custom-call(bf16[2560,256]{1,0:T(8,128)(2,1)S(1)} %cannon.1.source), custom_call_target="tpu_custom_call" | custom-call | tf_op jit(solution)/shard_map/pass_on/pallas_call | solution.py:234

commit v4 on v3

--- a/solution.py
+++ b/solution.py
@@ -10,9 +10,10 @@
 BLK = 128
 LEVELS = 32767.0
 TINY = 1e-33
+PLANE = 4
 B_WINDOW = 3
 R_WINDOW = 3
-B_PARTS = (4, 3, 2, 1)
+B_PARTS = (6, 4, 3, 2, 1)
 MESH = pl.DeviceIdType.MESH
 
 
@@ -24,8 +25,8 @@
 def kernel(
     group, parts,
     a_hbm, b_hbm, mask_a, mask_b, out_tile,
-    flags_a, flags_b, a_tile, b_own, b_send, b_recv, own_sum, code_send, code_recv, step_send, step_recv,
-    f_sem, a_sem, b_sem, bs_sem, br_sem, cs_sem, cr_sem, ss_sem, sr_sem,
+    flags_a, flags_b, a_tile, b_own, b_send, b_recv, own_sum, code_send, code_recv, step_send, step_recv, passing,
+    f_sem, a_sem, b_sem, bs_sem, br_sem, cs_sem, cr_sem, ss_sem, sr_sem, p_sem,
 ):
     n_row, n_col = lax.axis_size("row"), lax.axis_size("col")
     row, col = lax.axis_index("row"), lax.axis_index("col")
@@ -77,9 +78,29 @@
             device_id={"row": row, "col": left}, device_id_type=MESH,
         )
 
+    last_col, last_piece = n_col - 1, pieces - 1
+    relay = max(n_col - 2, 0)
+    hand_over = pltpu.make_async_remote_copy(
+        src_ref=b_send.at[last_piece], dst_ref=passing, send_sem=bs_sem.at[last_piece], recv_sem=p_sem.at[0],
+        device_id={"row": up, "col": relay}, device_id_type=MESH,
+    )
+    pass_along = pltpu.make_async_remote_copy(
+        src_ref=passing, dst_ref=b_recv.at[last_piece], send_sem=p_sem.at[1], recv_sem=br_sem.at[last_piece],
+        device_id={"row": row, "col": 0}, device_id_type=MESH,
+    )
+
     barrier = pltpu.get_barrier_semaphore()
     pl.semaphore_signal(barrier, inc=1, device_id={"row": down, "col": left}, device_id_type=MESH)
     pl.semaphore_signal(barrier, inc=1, device_id={"row": down, "col": col}, device_id_type=MESH)
+
+    @pl.when(col == 0)
+    def _():
+        pl.semaphore_signal(barrier, inc=1, device_id={"row": row, "col": relay}, device_id_type=MESH)
+
+    @pl.when(col == relay)
+    def _():
+        pl.semaphore_signal(barrier, inc=1, device_id={"row": down, "col": last_col}, device_id_type=MESH)
+
     get_flags_b.start()
     for n in range(pieces):
         load_send(n).start()
@@ -91,7 +112,7 @@
             lines = slice(k * BLK, (k + 1) * BLK)
             b_send[n, lines, :] = times_flag(b_send[n, lines, :], flags_b[h, slot * deep + p * (deep // parts) + k])
         if n == 0:
-            pl.semaphore_wait(barrier, 2)
+            pl.semaphore_wait(barrier, 2 + jnp.where(col == last_col, 1, 0) + jnp.where(col == relay, 1, 0))
         if n < b_window:
             move_b(n).start()
         if n == 0:
@@ -100,6 +121,11 @@
             for c in range(chunks):
                 load_a(c).start()
 
+
+    @pl.when(col == last_col)
+    def _():
+        hand_over.start()
+
     get_own.wait()
     for h in range(halves):
         for k in range(deep):
@@ -109,7 +135,11 @@
 
     def next_b(n, carry):
         move_b(n - b_window).wait_send()
-        move_b(n).start()
+
+        @pl.when((col != last_col) | (n != last_piece))
+        def _():
+            move_b(n).start()
+
         return carry
 
     def own_part(c, carry):
@@ -157,9 +187,28 @@
 
     for h in range(halves):
         if h == halves - 1:
+            hold = (lax.rem(col, PLANE) == 0) | (col == relay)
+
+            @pl.when(jnp.logical_not(hold))
+            def _():
+                lax.fori_loop(0, r_window, send_out, 0)
+
             for n in range(pieces - b_window, pieces):
                 move_b(n).wait_send()
-            lax.fori_loop(0, r_window, send_out, 0)
+
+            @pl.when(hold)
+            def _():
+                lax.fori_loop(0, 1, send_out, 0)
+
+            @pl.when(col == relay)
+            def _():
+                hand_over.wait_recv()
+                pass_along.start()
+
+            @pl.when(hold)
+            def _():
+                lax.fori_loop(1, r_window, send_out, 0)
+
         for n in range(h * parts, (h + 1) * parts):
             move_b(n).wait_recv()
         lax.fori_loop(0, chunks, functools.partial(next_part, h), 0)
@@ -179,6 +228,10 @@
 
         lax.fori_loop(0, chunks, finish, 0)
     lax.fori_loop(sends - r_window if r_window else 0, sends, sent, 0)
+
+    @pl.when(col == relay)
+    def _():
+        pass_along.wait_send()
 
 
 def pass_on(pieces, source, target, sem):
@@ -225,8 +278,9 @@
             pltpu.VMEM((sends, span, BLK), jnp.int16),
             pltpu.VMEM((sends, 1, BLK), jnp.float32),
             pltpu.VMEM((sends, 1, BLK), jnp.float32),
+            pltpu.VMEM((inner // parts, BLK), jnp.bfloat16),
             dma((2,)), dma((chunks,)), dma((pieces + 1,)), dma((pieces,)), dma((pieces,)),
-            dma((sends,)), dma((sends,)), dma((sends,)), dma((sends,)),
+            dma((sends,)), dma((sends,)), dma((sends,)), dma((sends,)), dma((2,)),
         ],
         compiler_params=pltpu.CompilerParams(collective_id=0, has_side_effects=True, vmem_limit_bytes=52 * 1024 * 1024),
         name="cannon",

time: 53.4 us -> 52.6 us (0.985)
  Pallas kernels: 53.2 us -> 51.9 us
    pallas_call x1, Pallas kernels: 52.1 us -> 50.8 us  [body(): pl.pallas_call(functools.partial(kernel, group, parts), out_shape=pltpu.V...]
where the time goes in v4:
time: 52.6 us; the launch traced here: 51.9 us
  Pallas kernels  51.9 us (99%)
    pallas_call x1, Pallas kernels, body(): pl.pallas_call(functools.partial(kernel, group, parts), out_shape=pltpu.V...  50.8 us
    pallas_call x1, Pallas kernels, body(): pl.pallas_call(functools.partial(pass_on, chunks), out_shape=jax.ShapeDty...  1.09 us

profile of v4, /device:TPU:5, one launch (start us, length us, event | category | flops | bytes accessed | tf_op | source)
XLA Modules:
  0.0 51.9 jit_solution(7049946712632142355)
XLA Ops:
  0.0 50.8 %cannon.1.source = bf16[2560,256]{1,0:T(8,128)(2,1)S(1)} custom-call(bf16[2560,1536]{1,0:T(8,128)(2,1)} %a_hbm.1, bf16[12288,256]{1,0:T(8,128)(2,1)} %b_hbm.1, s32[12,20]{1,0:T(8,128)} %bitcast.2, s32[2,96]{1,0:T(2,128)} %bitcast.3), custom_call_target="tpu_custom_call" | custom-call | tf_op jit(solution)/shard_map/cannon/pallas_call | solution.py:264
  50.8 1.1 %pass_on.1 = bf16[2560,256]{1,0:T(8,128)(2,1)} custom-call(bf16[2560,256]{1,0:T(8,128)(2,1)S(1)} %cannon.1.source), custom_call_target="tpu_custom_call" | custom-call | tf_op jit(solution)/shard_map/pass_on/pallas_call | solution.py:288

commit v5 on v4

--- a/solution.py
+++ b/solution.py
@@ -11,10 +11,32 @@
 LEVELS = 32767.0
 TINY = 1e-33
 PLANE = 4
-B_WINDOW = 3
-R_WINDOW = 3
 B_PARTS = (6, 4, 3, 2, 1)
 MESH = pl.DeviceIdType.MESH
+
+
+def runs(start, sizes):
+    found = []
+    for size in sizes:
+        if size > 0:
+            found.append((start, size))
+        start += size
+    return found
+
+
+def b_runs(halves, parts):
+    found = []
+    for h in range(halves - 1):
+        found += runs(h * parts, (parts // 2, parts - parts // 2))
+    return found + runs((halves - 1) * parts, (parts - 1, 1))
+
+
+def r_runs(halves, chunks):
+    first = max(2 * chunks // 5, 1)
+    found = []
+    for h in range(halves - 1):
+        found += runs(h * chunks, (first, chunks - first))
+    return found, runs((halves - 1) * chunks, (chunks - 1, 1))
 
 
 def times_flag(block, flag):
@@ -39,8 +61,8 @@
     chunks = rows // span
     cut = inner // parts
     pieces, sends = halves * parts, halves * chunks
-    ready = sends - chunks
-    b_window, r_window = min(B_WINDOW, pieces), min(R_WINDOW, ready)
+    b_parts, (r_early, r_late) = b_runs(halves, parts), r_runs(halves, chunks)
+    r_parts = r_early + r_late
 
     def lines_of(c):
         return pl.ds(pl.multiple_of(c * span, span), span)
@@ -60,32 +82,38 @@
     get_flags_b = pltpu.make_async_copy(mask_b, flags_b, f_sem.at[0])
     get_flags_a = pltpu.make_async_copy(mask_a, flags_a, f_sem.at[1])
 
-    def move_b(n):
+    def move_b(j):
+        start, size = b_parts[j]
+        spot = slice(start, start + size)
         return pltpu.make_async_remote_copy(
-            src_ref=b_send.at[n], dst_ref=b_recv.at[n], send_sem=bs_sem.at[n], recv_sem=br_sem.at[n],
+            src_ref=b_send.at[spot], dst_ref=b_recv.at[spot], send_sem=bs_sem.at[j], recv_sem=br_sem.at[j],
             device_id={"row": up, "col": right}, device_id_type=MESH,
         )
 
-    def move_code(i):
+    def move_code(j):
+        start, size = r_parts[j]
+        spot = slice(start, start + size)
         return pltpu.make_async_remote_copy(
-            src_ref=code_send.at[i], dst_ref=code_recv.at[i], send_sem=cs_sem.at[i], recv_sem=cr_sem.at[i],
+            src_ref=code_send.at[spot], dst_ref=code_recv.at[spot], send_sem=cs_sem.at[j], recv_sem=cr_sem.at[j],
             device_id={"row": row, "col": left}, device_id_type=MESH,
         )
 
-    def move_step(i):
+    def move_step(h):
+        spot = slice(h * chunks, (h + 1) * chunks)
         return pltpu.make_async_remote_copy(
-            src_ref=step_send.at[i], dst_ref=step_recv.at[i], send_sem=ss_sem.at[i], recv_sem=sr_sem.at[i],
+            src_ref=step_send.at[spot], dst_ref=step_recv.at[spot], send_sem=ss_sem.at[h], recv_sem=sr_sem.at[h],
             device_id={"row": row, "col": left}, device_id_type=MESH,
         )
 
-    last_col, last_piece = n_col - 1, pieces - 1
+    last_col, last_part = n_col - 1, len(b_parts) - 1
+    tail = slice(b_parts[-1][0], pieces)
     relay = max(n_col - 2, 0)
     hand_over = pltpu.make_async_remote_copy(
-        src_ref=b_send.at[last_piece], dst_ref=passing, send_sem=bs_sem.at[last_piece], recv_sem=p_sem.at[0],
+        src_ref=b_send.at[tail], dst_ref=passing, send_sem=bs_sem.at[last_part], recv_sem=p_sem.at[0],
         device_id={"row": up, "col": relay}, device_id_type=MESH,
     )
     pass_along = pltpu.make_async_remote_copy(
-        src_ref=passing, dst_ref=b_recv.at[last_piece], send_sem=p_sem.at[1], recv_sem=br_sem.at[last_piece],
+        src_ref=passing, dst_ref=b_recv.at[tail], send_sem=p_sem.at[1], recv_sem=br_sem.at[last_part],
         device_id={"row": row, "col": 0}, device_id_type=MESH,
     )
 
@@ -111,16 +139,20 @@
         for k in range(deep // parts):
             lines = slice(k * BLK, (k + 1) * BLK)
             b_send[n, lines, :] = times_flag(b_send[n, lines, :], flags_b[h, slot * deep + p * (deep // parts) + k])
-        if n == 0:
+        done = [start + size for start, size in b_parts]
+        if n + 1 == done[0]:
             pl.semaphore_wait(barrier, 2 + jnp.where(col == last_col, 1, 0) + jnp.where(col == relay, 1, 0))
-        if n < b_window:
-            move_b(n).start()
-        if n == 0:
+        if n + 1 in done[:-1]:
+            move_b(done.index(n + 1)).start()
+        if n + 1 == done[0]:
             get_flags_a.start()
             get_own.start()
             for c in range(chunks):
                 load_a(c).start()
 
+    @pl.when(col != last_col)
+    def _():
+        move_b(last_part).start()
 
     @pl.when(col == last_col)
     def _():
@@ -132,15 +164,6 @@
             spot = (slice(k * BLK, (k + 1) * BLK), slice(h * BLK, (h + 1) * BLK))
             b_own[spot] = times_flag(b_own[spot], flags_b[h, k])
     get_flags_a.wait()
-
-    def next_b(n, carry):
-        move_b(n - b_window).wait_send()
-
-        @pl.when((col != last_col) | (n != last_piece))
-        def _():
-            move_b(n).start()
-
-        return carry
 
     def own_part(c, carry):
         load_a(c).wait()
@@ -150,29 +173,13 @@
                 block = a_tile[lines, k * BLK:(k + 1) * BLK]
                 a_tile[lines, k * BLK:(k + 1) * BLK] = times_flag(block, flags_a[k, c * group + g])
         own_sum[lines_of(c), :] = jnp.dot(a_tile[lines_of(c), :], b_own[...], preferred_element_type=jnp.float32)
-
-        @pl.when(b_window + c < pieces)
-        def _():
-            next_b(b_window + c, 0)
-
         return carry
 
     lax.fori_loop(0, chunks, own_part, 0)
-    lax.fori_loop(min(b_window + chunks, pieces), pieces, next_b, 0)
-
-    def send_out(i, carry):
-        move_step(i).start()
-        move_code(i).start()
-        return carry
-
-    def sent(i, carry):
-        move_step(i).wait_send()
-        move_code(i).wait_send()
-        return carry
-
-    def next_out(i, carry):
-        sent(i - r_window, carry)
-        return send_out(i, carry)
+
+    def send_out(first, last):
+        for j in range(first, last):
+            move_code(j).start()
 
     def next_part(h, c, carry):
         i = h * chunks + c
@@ -181,24 +188,23 @@
         most = jnp.maximum(jnp.max(jnp.abs(value), axis=0, keepdims=True), TINY)
         step_send[i] = most * (1.0 / LEVELS)
         code_send[i] = jnp.round(value * (LEVELS / most)).astype(jnp.int32).astype(jnp.int16)
-        if h < halves - 1:
-            return carry
-        return next_out(r_window + c, carry) if r_window else send_out(c, carry)
-
+        return carry
+
+    early = len(r_early)
+    hold = (lax.rem(col, PLANE) == 0) | (col == relay)
     for h in range(halves):
         if h == halves - 1:
-            hold = (lax.rem(col, PLANE) == 0) | (col == relay)
 
             @pl.when(jnp.logical_not(hold))
             def _():
-                lax.fori_loop(0, r_window, send_out, 0)
-
-            for n in range(pieces - b_window, pieces):
-                move_b(n).wait_send()
+                send_out(0, early)
+
+            for j in range(len(b_parts)):
+                move_b(j).wait_send()
 
             @pl.when(hold)
             def _():
-                lax.fori_loop(0, 1, send_out, 0)
+                send_out(0, 1)
 
             @pl.when(col == relay)
             def _():
@@ -207,27 +213,34 @@
 
             @pl.when(hold)
             def _():
-                lax.fori_loop(1, r_window, send_out, 0)
-
-        for n in range(h * parts, (h + 1) * parts):
-            move_b(n).wait_recv()
+                send_out(1, early)
+
+        for j, (start, _) in enumerate(b_parts):
+            if start // parts == h:
+                move_b(j).wait_recv()
         lax.fori_loop(0, chunks, functools.partial(next_part, h), 0)
-    if r_window:
-        lax.fori_loop(r_window + chunks, sends, next_out, 0)
-
-    for h in range(halves):
+        move_step(h).start()
+    send_out(early, len(r_parts))
+
+    for j, (start, size) in enumerate(r_parts):
+        h = start // chunks
 
         def finish(c, carry, h=h):
             i = h * chunks + c
-            move_step(i).wait_recv()
-            move_code(i).wait_recv()
             code = code_recv[i].astype(jnp.int32).astype(jnp.float32)
             total = own_sum[lines_of(c), h * BLK:(h + 1) * BLK] + code * step_recv[i]
             out_tile[lines_of(c), h * BLK:(h + 1) * BLK] = total.astype(out_tile.dtype)
             return carry
 
-        lax.fori_loop(0, chunks, finish, 0)
-    lax.fori_loop(sends - r_window if r_window else 0, sends, sent, 0)
+        if start == h * chunks:
+            move_step(h).wait_recv()
+        move_code(j).wait_recv()
+        lax.fori_loop(start - h * chunks, start - h * chunks + size, finish, 0)
+
+    for h in range(halves):
+        move_step(h).wait_send()
+    for j in range(len(r_parts)):
+        move_code(j).wait_send()
 
     @pl.when(col == relay)
     def _():
@@ -260,6 +273,7 @@
     chunks = rows // span
     halves = width // BLK
     pieces, sends = halves * parts, halves * chunks
+    b_copies, r_copies = len(b_runs(halves, parts)), sum(map(len, r_runs(halves, chunks)))
     dma = pltpu.SemaphoreType.DMA
     product = pl.pallas_call(
         functools.partial(kernel, group, parts),
@@ -278,9 +292,9 @@
             pltpu.VMEM((sends, span, BLK), jnp.int16),
             pltpu.VMEM((sends, 1, BLK), jnp.float32),
             pltpu.VMEM((sends, 1, BLK), jnp.float32),
-            pltpu.VMEM((inner // parts, BLK), jnp.bfloat16),
-            dma((2,)), dma((chunks,)), dma((pieces + 1,)), dma((pieces,)), dma((pieces,)),
-            dma((sends,)), dma((sends,)), dma((sends,)), dma((sends,)), dma((2,)),
+            pltpu.VMEM((1, inner // parts, BLK), jnp.bfloat16),
+            dma((2,)), dma((chunks,)), dma((pieces + 1,)), dma((b_copies,)), dma((b_copies,)),
+            dma((r_copies,)), dma((r_copies,)), dma((halves,)), dma((halves,)), dma((2,)),
         ],
         compiler_params=pltpu.CompilerParams(collective_id=0, has_side_effects=True, vmem_limit_bytes=52 * 1024 * 1024),
         name="cannon",

time: 52.6 us -> 52.1 us (level)
  no operation moved by 1% of the time
where the time goes in v5:
time: 52.1 us; the launch traced here: 51.5 us
  Pallas kernels  51.5 us (99%)
    pallas_call x1, Pallas kernels, body(): pl.pallas_call(functools.partial(kernel, group, parts), out_shape=pltpu.V...  50.4 us
    pallas_call x1, Pallas kernels, body(): pl.pallas_call(functools.partial(pass_on, chunks), out_shape=jax.ShapeDty...  1.09 us

profile of v5, /device:TPU:5, one launch (start us, length us, event | category | flops | bytes accessed | tf_op | source)
XLA Modules:
  0.0 51.5 jit_solution(2533590524529152918)
XLA Ops:
  0.0 50.4 %cannon.1.source = bf16[2560,256]{1,0:T(8,128)(2,1)S(1)} custom-call(bf16[2560,1536]{1,0:T(8,128)(2,1)} %a_hbm.1, bf16[12288,256]{1,0:T(8,128)(2,1)} %b_hbm.1, s32[12,20]{1,0:T(8,128)} %bitcast.2, s32[2,96]{1,0:T(2,128)} %bitcast.3), custom_call_target="tpu_custom_call" | custom-call | tf_op jit(solution)/shard_map/cannon/pallas_call | solution.py:278
  50.4 1.1 %pass_on.1 = bf16[2560,256]{1,0:T(8,128)(2,1)} custom-call(bf16[2560,256]{1,0:T(8,128)(2,1)S(1)} %cannon.1.source), custom_call_target="tpu_custom_call" | custom-call | tf_op jit(solution)/shard_map/pass_on/pallas_call | solution.py:302

commit v6 on v5

--- a/solution.py
+++ b/solution.py
@@ -11,7 +11,8 @@
 LEVELS = 32767.0
 TINY = 1e-33
 PLANE = 4
-B_PARTS = (6, 4, 3, 2, 1)
+WAYS = 2
+B_PARTS = (12, 6, 4, 3, 2, 1)
 MESH = pl.DeviceIdType.MESH
 
 
@@ -28,7 +29,7 @@
     found = []
     for h in range(halves - 1):
         found += runs(h * parts, (parts // 2, parts - parts // 2))
-    return found + runs((halves - 1) * parts, (parts - 1, 1))
+    return found + runs((halves - 1) * parts, (parts - WAYS,) + (1,) * WAYS)
 
 
 def r_runs(halves, chunks):
@@ -105,29 +106,46 @@
             device_id={"row": row, "col": left}, device_id_type=MESH,
         )
 
-    last_col, last_part = n_col - 1, len(b_parts) - 1
-    tail = slice(b_parts[-1][0], pieces)
-    relay = max(n_col - 2, 0)
-    hand_over = pltpu.make_async_remote_copy(
-        src_ref=b_send.at[tail], dst_ref=passing, send_sem=bs_sem.at[last_part], recv_sem=p_sem.at[0],
-        device_id={"row": up, "col": relay}, device_id_type=MESH,
-    )
-    pass_along = pltpu.make_async_remote_copy(
-        src_ref=passing, dst_ref=b_recv.at[tail], send_sem=p_sem.at[1], recv_sem=br_sem.at[last_part],
-        device_id={"row": row, "col": 0}, device_id_type=MESH,
-    )
+    common = len(b_parts) - WAYS
+    detours = ((n_col - 1, n_col - 2, (0, 1), None), (1, 2 * PLANE + 2, (0, 1), 0))
+
+    def at_source(source, line):
+        return col == source if line is None else (col == source) & (row == line)
+
+    def beyond(column, line):
+        return col == column if line is None else (col == column) & (row == (line + n_row - 1) % n_row)
+
+    def first_leg(relay, w):
+        start, size = b_parts[common + w]
+        return pltpu.make_async_remote_copy(
+            src_ref=b_send.at[start:start + size], dst_ref=passing.at[w:w + size],
+            send_sem=bs_sem.at[common + w], recv_sem=p_sem.at[w],
+            device_id={"row": up, "col": relay}, device_id_type=MESH,
+        )
+
+    def second_leg(source, w):
+        start, size = b_parts[common + w]
+        return pltpu.make_async_remote_copy(
+            src_ref=passing.at[w:w + size], dst_ref=b_recv.at[start:start + size],
+            send_sem=p_sem.at[WAYS + w], recv_sem=br_sem.at[common + w],
+            device_id={"row": row, "col": (source + 1) % n_col}, device_id_type=MESH,
+        )
 
     barrier = pltpu.get_barrier_semaphore()
     pl.semaphore_signal(barrier, inc=1, device_id={"row": down, "col": left}, device_id_type=MESH)
     pl.semaphore_signal(barrier, inc=1, device_id={"row": down, "col": col}, device_id_type=MESH)
 
-    @pl.when(col == 0)
-    def _():
-        pl.semaphore_signal(barrier, inc=1, device_id={"row": row, "col": relay}, device_id_type=MESH)
-
-    @pl.when(col == relay)
-    def _():
-        pl.semaphore_signal(barrier, inc=1, device_id={"row": down, "col": last_col}, device_id_type=MESH)
+    greets = 2
+    for source, relay, _, line in detours:
+        greets += jnp.where(at_source(source, line), 1, 0) + jnp.where(beyond(relay, line), 1, 0)
+
+        @pl.when(beyond((source + 1) % n_col, line))
+        def _(relay=relay):
+            pl.semaphore_signal(barrier, inc=1, device_id={"row": row, "col": relay}, device_id_type=MESH)
+
+        @pl.when(beyond(relay, line))
+        def _(source=source):
+            pl.semaphore_signal(barrier, inc=1, device_id={"row": down, "col": source}, device_id_type=MESH)
 
     get_flags_b.start()
     for n in range(pieces):
@@ -141,8 +159,8 @@
             b_send[n, lines, :] = times_flag(b_send[n, lines, :], flags_b[h, slot * deep + p * (deep // parts) + k])
         done = [start + size for start, size in b_parts]
         if n + 1 == done[0]:
-            pl.semaphore_wait(barrier, 2 + jnp.where(col == last_col, 1, 0) + jnp.where(col == relay, 1, 0))
-        if n + 1 in done[:-1]:
+            pl.semaphore_wait(barrier, greets)
+        if n + 1 in done[:common]:
             move_b(done.index(n + 1)).start()
         if n + 1 == done[0]:
             get_flags_a.start()
@@ -150,13 +168,19 @@
             for c in range(chunks):
                 load_a(c).start()
 
-    @pl.when(col != last_col)
-    def _():
-        move_b(last_part).start()
-
-    @pl.when(col == last_col)
-    def _():
-        hand_over.start()
+    for w in range(WAYS):
+        straight = True
+        for source, relay, ways, line in detours:
+            if w in ways:
+                straight &= jnp.logical_not(at_source(source, line))
+
+                @pl.when(at_source(source, line))
+                def _(relay=relay, w=w):
+                    first_leg(relay, w).start()
+
+        @pl.when(straight)
+        def _(w=w):
+            move_b(common + w).start()
 
     get_own.wait()
     for h in range(halves):
@@ -191,7 +215,9 @@
         return carry
 
     early = len(r_early)
-    hold = (lax.rem(col, PLANE) == 0) | (col == relay)
+    hold = lax.rem(col, PLANE) == 0
+    for _, relay, _, line in detours:
+        hold |= beyond(relay, line)
     for h in range(halves):
         if h == halves - 1:
 
@@ -206,10 +232,13 @@
             def _():
                 send_out(0, 1)
 
-            @pl.when(col == relay)
-            def _():
-                hand_over.wait_recv()
-                pass_along.start()
+            for source, relay, ways, line in detours:
+
+                @pl.when(beyond(relay, line))
+                def _(source=source, relay=relay, ways=ways):
+                    for w in ways:
+                        first_leg(relay, w).wait_recv()
+                        second_leg(source, w).start()
 
             @pl.when(hold)
             def _():
@@ -242,9 +271,12 @@
     for j in range(len(r_parts)):
         move_code(j).wait_send()
 
-    @pl.when(col == relay)
-    def _():
-        pass_along.wait_send()
+    for source, relay, ways, line in detours:
+
+        @pl.when(beyond(relay, line))
+        def _(source=source, ways=ways):
+            for w in ways:
+                second_leg(source, w).wait_send()
 
 
 def pass_on(pieces, source, target, sem):
@@ -292,9 +324,9 @@
             pltpu.VMEM((sends, span, BLK), jnp.int16),
             pltpu.VMEM((sends, 1, BLK), jnp.float32),
             pltpu.VMEM((sends, 1, BLK), jnp.float32),
-            pltpu.VMEM((1, inner // parts, BLK), jnp.bfloat16),
+            pltpu.VMEM((WAYS, inner // parts, BLK), jnp.bfloat16),
             dma((2,)), dma((chunks,)), dma((pieces + 1,)), dma((b_copies,)), dma((b_copies,)),
-            dma((r_copies,)), dma((r_copies,)), dma((halves,)), dma((halves,)), dma((2,)),
+            dma((r_copies,)), dma((r_copies,)), dma((halves,)), dma((halves,)), dma((2 * WAYS,)),
         ],
         compiler_params=pltpu.CompilerParams(collective_id=0, has_side_effects=True, vmem_limit_bytes=52 * 1024 * 1024),
         name="cannon",

time: 52.1 us -> 51.9 us (level)
  no operation moved by 1% of the time
where the time goes in v6:
time: 51.9 us; the launch traced here: 51.7 us
  Pallas kernels  51.7 us (100%)
    pallas_call x1, Pallas kernels, body(): pl.pallas_call(functools.partial(kernel, group, parts), out_shape=pltpu.V...  50.6 us
    pallas_call x1, Pallas kernels, body(): pl.pallas_call(functools.partial(pass_on, chunks), out_shape=jax.ShapeDty...  1.09 us

profile of v6, /device:TPU:5, one launch (start us, length us, event | category | flops | bytes accessed | tf_op | source)
XLA Modules:
  0.0 51.7 jit_solution(2726352566566858875)
XLA Ops:
  0.0 50.6 %cannon.1.source = bf16[2560,256]{1,0:T(8,128)(2,1)S(1)} custom-call(bf16[2560,1536]{1,0:T(8,128)(2,1)} %a_hbm.1, bf16[12288,256]{1,0:T(8,128)(2,1)} %b_hbm.1, s32[12,20]{1,0:T(8,128)} %bitcast.2, s32[2,96]{1,0:T(2,128)} %bitcast.3), custom_call_target="tpu_custom_call" | custom-call | tf_op jit(solution)/shard_map/cannon/pallas_call | solution.py:310
  50.6 1.1 %pass_on.1 = bf16[2560,256]{1,0:T(8,128)(2,1)} custom-call(bf16[2560,256]{1,0:T(8,128)(2,1)S(1)} %cannon.1.source), custom_call_target="tpu_custom_call" | custom-call | tf_op jit(solution)/shard_map/pass_on/pallas_call | solution.py:334

commit v7 on v6

--- a/solution.py
+++ b/solution.py
@@ -28,7 +28,7 @@
 def b_runs(halves, parts):
     found = []
     for h in range(halves - 1):
-        found += runs(h * parts, (parts // 2, parts - parts // 2))
+        found += runs(h * parts, (parts,))
     return found + runs((halves - 1) * parts, (parts - WAYS,) + (1,) * WAYS)
 
 
@@ -299,7 +299,7 @@
     rows, inner = mat_a.shape
     width = mat_b.shape[1]
     block_rows = mask_a.shape[0]
-    group = next(g for g in (4, 2, 1) if block_rows % g == 0)
+    group = next(g for g in (5, 4, 2, 1) if block_rows % g == 0)
     parts = next(p for p in B_PARTS if inner // BLK % p == 0)
     span = group * BLK
     chunks = rows // span

time: 51.9 us -> 51.9 us (level)
  no operation moved by 1% of the time
where the time goes in v7:
time: 51.9 us; the launch traced here: 51.7 us
  Pallas kernels  51.7 us (100%)
    pallas_call x1, Pallas kernels, body(): pl.pallas_call(functools.partial(kernel, group, parts), out_shape=pltpu.V...  50.6 us
    pallas_call x1, Pallas kernels, body(): pl.pallas_call(functools.partial(pass_on, chunks), out_shape=jax.ShapeDty...  1.08 us

profile of v7, /device:TPU:5, one launch (start us, length us, event | category | flops | bytes accessed | tf_op | source)
XLA Modules:
  0.0 51.7 jit_solution(16383273596561359021)
XLA Ops:
  0.0 50.6 %cannon.1.source = bf16[2560,256]{1,0:T(8,128)(2,1)S(1)} custom-call(bf16[2560,1536]{1,0:T(8,128)(2,1)} %a_hbm.1, bf16[12288,256]{1,0:T(8,128)(2,1)} %b_hbm.1, s32[12,20]{1,0:T(8,128)} %bitcast.2, s32[2,96]{1,0:T(2,128)} %bitcast.3), custom_call_target="tpu_custom_call" | custom-call | tf_op jit(solution)/shard_map/cannon/pallas_call | solution.py:310
  50.6 1.1 %pass_on.1 = bf16[2560,256]{1,0:T(8,128)(2,1)} custom-call(bf16[2560,256]{1,0:T(8,128)(2,1)S(1)} %cannon.1.source), custom_call_target="tpu_custom_call" | custom-call | tf_op jit(solution)/shard_map/pass_on/pallas_call | solution.py:334

commit v8 on v6

--- a/solution.py
+++ b/solution.py
@@ -11,7 +11,7 @@
 LEVELS = 32767.0
 TINY = 1e-33
 PLANE = 4
-WAYS = 2
+WAYS = 3
 B_PARTS = (12, 6, 4, 3, 2, 1)
 MESH = pl.DeviceIdType.MESH
 
@@ -107,7 +107,7 @@
         )
 
     common = len(b_parts) - WAYS
-    detours = ((n_col - 1, n_col - 2, (0, 1), None), (1, 2 * PLANE + 2, (0, 1), 0))
+    detours = ((n_col - 1, n_col - 2, (0, 1, 2), 1), (n_col - 1, PLANE + 2, (1, 2), 0), (1, 2 * PLANE + 2, (1, 2), 1))
 
     def at_source(source, line):
         return col == source if line is None else (col == source) & (row == line)

time: 51.9 us -> 51.9 us (level)
  no operation moved by 1% of the time
where the time goes in v8:
time: 51.9 us; the launch traced here: 51.4 us
  Pallas kernels  51.4 us (99%)
    pallas_call x1, Pallas kernels, body(): pl.pallas_call(functools.partial(kernel, group, parts), out_shape=pltpu.V...  50.3 us
    pallas_call x1, Pallas kernels, body(): pl.pallas_call(functools.partial(pass_on, chunks), out_shape=jax.ShapeDty...  1.09 us

profile of v8, /device:TPU:5, one launch (start us, length us, event | category | flops | bytes accessed | tf_op | source)
XLA Modules:
  0.0 51.4 jit_solution(16674642485663474631)
XLA Ops:
  0.0 50.3 %cannon.1.source = bf16[2560,256]{1,0:T(8,128)(2,1)S(1)} custom-call(bf16[2560,1536]{1,0:T(8,128)(2,1)} %a_hbm.1, bf16[12288,256]{1,0:T(8,128)(2,1)} %b_hbm.1, s32[12,20]{1,0:T(8,128)} %bitcast.2, s32[2,96]{1,0:T(2,128)} %bitcast.3), custom_call_target="tpu_custom_call" | custom-call | tf_op jit(solution)/shard_map/cannon/pallas_call | solution.py:310
  50.3 1.1 %pass_on.1 = bf16[2560,256]{1,0:T(8,128)(2,1)} custom-call(bf16[2560,256]{1,0:T(8,128)(2,1)S(1)} %cannon.1.source), custom_call_target="tpu_custom_call" | custom-call | tf_op jit(solution)/shard_map/pass_on/pallas_call | solution.py:334
